TPU v7x, 32 devices: a whole 2x2x4 slice. The times are simulated.
32 devices in a mesh: grp: 8 (over y, x, core), top: 4 (over z).
Axes of the slice: x: 2, y: 2, z: 4, core: 2. Of those that a mesh axis runs over, the one named last changes fastest.
Arguments:
- basis_grad: float32 [8, 4, 512, 384], P('grp', 'top'), may hold values from -6 to 6
- leaf_q: float32 [8, 4, 512, 384], P('grp', 'top'), may hold values from -0.25 to 0.25
- leaf_rinv: float32 [8, 4, 384, 384], P('grp', 'top'), may hold values from -5 to 4, as said below
- merge_q1: float32 [8, 4, 384, 384], P('grp', 'top'), may hold values from -0.3125 to 0.3125
- merge_q2: float32 [4, 384, 384], P('top', 'grp'), may hold values from -0.15625 to 0.15625
Outputs:
- data_grad: float32 [8, 4, 512, 384], P('grp', 'top')
Inputs may be any that keep to these rules, and one draw needn't show every extreme that they name: Each leaf_rinv[i,g] is upper triangular with a diagonal between 1 and 4.
All inputs are finite; a program needn't handle non-finite values.
Results may differ from a plain program's by a relative error of at most 0.00023.
Values sent between devices are 32-bit elements; how exact they have to be, the bound alone decides.
A program may use at most 64 MiB of HBM per device.

v0:
```python
import jax
import jax.numpy as jnp
from jax import lax
from jax.sharding import PartitionSpec as P


def product(former, latter, former_dim, latter_dim):
    return lax.dot_general(
        former,
        latter,
        (((former_dim,), (latter_dim,)), ((), ())),
        precision=lax.Precision.HIGH,
        preferred_element_type=jnp.float32,
    )


def symmetrize(matrix):
    return jnp.tril(matrix) + jnp.tril(matrix, -1).T


def per_device(basis_grad, leaf_q, leaf_rinv, merge_q1, merge_q2):
    cotangent = basis_grad[0, 0]
    leaf_basis = leaf_q[0, 0]
    inverse = leaf_rinv[0, 0]
    first_block = merge_q1[0, 0]
    second_factor = lax.all_gather(merge_q2[0], "grp", axis=0, tiled=True)
    projected = product(leaf_basis, cotangent, 0, 0)
    combined = product(first_block, second_factor, 1, 0)
    top_adjoint = -lax.psum(product(projected, combined, 0, 0), ("grp", "top"))
    top_sym = symmetrize(top_adjoint)
    spread = product(leaf_basis, combined, 1, 0)
    outer = product(inverse, combined, 1, 0)
    inner = cotangent + product(spread, top_sym, 1, 0)
    result = product(inner, outer, 1, 1)
    return result[None, None]


def solution(mesh):
    placed = (
        P("grp", "top", None, None),
        P("grp", "top", None, None),
        P("grp", "top", None, None),
        P("grp", "top", None, None),
        P("top", "grp", None),
    )
    return jax.shard_map(
        per_device,
        mesh=mesh,
        in_specs=placed,
        out_specs=P("grp", "top", None, None),
        check_vma=False,
    )
```

profile of v0, /device:TPU:0, one launch (start us, length us, event | category | flops | bytes accessed | tf_op | source)
XLA Modules:
  0.0 163.3 jit_solution(13517483141683757118)
XLA Ops:
  6.5 0.0 copy-start
  6.5 0.0 copy-start.2
  6.5 0.0 all-reduce.2.cloned.1.call-start
  6.5 11.9 %all-gather = f32[1,384,384]{2,1,0:T(8,128)S(1)} all-gather(f32[1,48,384]{2,1,0:T(8,128)} %param.9), channel_id=2, replica_groups=mesh['grp'=8,'top'=4] {'grp'}, dimensions={1}, use_global_device_ids=true | all-gather | bytes 663552 | tf_op jit(solution)/shard_map/all_gather | solution.py:26
  18.4 0.0 copy-done.2
  18.4 0.0 copy-start.1
  18.4 0.7 fusion.7
  19.2 0.0 copy-done
  19.2 0.4 copy-done.1
  19.6 0.8 fusion
  20.4 1.6 fusion.17
  22.0 0.0 copy-start.3
  22.0 0.0 all-reduce.2.cloned.1.call-update
  22.0 1.0 copy-done.3
  23.0 1.1 fusion.5
  24.2 1.2 fusion.2
  25.3 124.4 %all-reduce.2.cloned.1.call-done = f32[384,384]{1,0:T(8,128)} async-done(((f32[384,384]{1,0:T(8,128)}), f32[384,384]{1,0:T(8,128)}) %all-reduce.2.cloned.1.call-update) | async-done | bytes 589840 | tf_op jit(solution)/shard_map/psum | solution.py:29
  149.8 1.1 neg.3
  150.9 1.1 copy.6
  151.9 2.7 %convolution_add_fusion = f32[512,384]{1,0:T(8,128)S(1)} fusion(f32[384,512]{1,0:T(8,128)S(1)} %fusion.2, f32[1,1,512,384]{3,2,1,0:T(8,128)S(1)} %copy-done.1, f32[384,384]{0,1:T(8,128)} %copy.6, s32[384]{0:T(512)S(1)} %iota_add_fusion, f32[384,384]{1,0:T(8,128)} %all-reduce.2.cloned.1.call-done), kind=kOutput, calls=%fused_computation.1 | convolution fusion | flops 454066176 | bytes 3540480 | tf_op jit(solution)/shard_map/dot_general | solution.py:8
  154.7 1.8 %convolution_bitcast_fusion = f32[1,1,512,384]{3,2,1,0:T(8,128)} fusion(f32[512,384]{1,0:T(8,128)S(1)} %convolution_add_fusion, f32[384,384]{1,0:T(8,128)S(1)} %fusion.5), kind=kOutput, calls=%fused_computation | convolution fusion | flops 452984832 | bytes 2162688 | tf_op jit(solution)/shard_map/dot_general | solution.py:8
  (1 shorter events, 0.0 us)
Async XLA Ops:
  6.5 12.6 %copy-start = (f32[1,1,512,384]{3,2,1,0:T(8,128)S(1)}, f32[1,1,512,384]{3,2,1,0:T(8,128)}, u32[]{:S(2)}) copy-start(f32[1,1,512,384]{3,2,1,0:T(8,128)} %param.6) | copy-start | bytes 2359300
  6.5 11.9 %copy-start.2 = (f32[1,1,384,384]{3,2,1,0:T(8,128)S(1)}, f32[1,1,384,384]{3,2,1,0:T(8,128)}, u32[]{:S(2)}) copy-start(f32[1,1,384,384]{3,2,1,0:T(8,128)} %param.8) | copy-start | bytes 1769476
  6.5 143.2 %all-reduce.2.cloned.1.call-start = ((), (), s32[]{:S(2)}) async-start(), calls=%async_computation | async-start | bytes 1179648 | tf_op jit(solution)/shard_map/psum | solution.py:29
  18.4 1.1 copy-start.1
  22.0 1.1 copy-start.3
Sparse Core Ops, SparseCore 0:
  22.1 127.6 all-reduce.1
where the time goes:
time: 164 us; the launch traced here: 163 us
  waiting for transfers between devices  124 us (76%)
  between operations  13.4 us (8%)
  blocking collectives  11.9 us (7%)
  matrix products  9.86 us (6%)
  local copies, waits for them, and re-layouts  2.51 us (2%)
    psum x1, waiting for transfers between devices, per_device(): top_adjoint = -lax.psum(product(projected, combined, 0, 0), ('grp', 'top'))  124 us
    all_gather x1, blocking collectives, per_device(): second_factor = lax.all_gather(merge_q2[0], 'grp', axis=0, tiled=True)  11.9 us
    dot_general x7, matrix products, product(): lax.dot_general(former, latter, (((former_dim,), (latter_dim,)), ((), ())...  9.86 us
  transfers between devices with their start and end apart: 1, of which 1 were waited for; matrix products, arithmetic and copies ran while one was open for 1% of the time, Pallas kernels for 0%

commit v1 on v0

--- a/solution.py
+++ b/solution.py
@@ -1,7 +1,38 @@
+import functools
 import jax
 import jax.numpy as jnp
 from jax import lax
 from jax.sharding import PartitionSpec as P
+
+
+def _produce_case(s0, at_axis):
+    r_now = lax.axis_size("grp")
+    after = lax.axis_index("grp")
+    prior, back, z = (r_now, after, s0.shape[at_axis])
+    table = []
+    for u in range(prior):
+        table.append((u, (u + 1) % prior))
+    blocks_here = []
+    for u in range(prior):
+        blocks_here.append((u, (u - 1) % prior))
+    ready = jnp.zeros((*s0.shape[:at_axis], prior * z, *s0.shape[at_axis + 1 :]), s0.dtype)
+    ready = lax.dynamic_update_slice_in_dim(ready, s0, back * z, axis=at_axis)
+    all_values = finding = s0
+    s_next = prior // 2
+    for rr in range(1, s_next + 1):
+        all_values = lax.ppermute(all_values, axis_name="grp", perm=table)
+        ready = lax.dynamic_update_slice_in_dim(
+            ready, all_values, (back - rr) % prior * z, axis=at_axis
+        )
+        if rr < prior - s_next:
+            finding = lax.ppermute(finding, axis_name="grp", perm=blocks_here)
+            ready = lax.dynamic_update_slice_in_dim(
+                ready, finding, (back + rr) % prior * z, axis=at_axis
+            )
+    return ready
+
+
+move_masks = functools.partial(_produce_case, at_axis=0)
 
 
 def product(former, latter, former_dim, latter_dim):
@@ -23,7 +54,7 @@
     leaf_basis = leaf_q[0, 0]
     inverse = leaf_rinv[0, 0]
     first_block = merge_q1[0, 0]
-    second_factor = lax.all_gather(merge_q2[0], "grp", axis=0, tiled=True)
+    second_factor = move_masks(merge_q2[0])
     projected = product(leaf_basis, cotangent, 0, 0)
     combined = product(first_block, second_factor, 1, 0)
     top_adjoint = -lax.psum(product(projected, combined, 0, 0), ("grp", "top"))

time: 164 us -> 189 us (1.15)
  local copies, waits for them, and re-layouts: 2.51 us -> 16.8 us
  waiting for transfers between devices: 124 us -> 137 us
  blocking collectives: 11.9 us -> 0 us
  starting transfers between devices: 0.01 us -> 8.69 us
    dynamic_update_slice x0 -> x8, local copies, waits for them, and re-layouts: none -> 13.5 us  [the longest x4 6.02 us: _produce_case(): lax.dynamic_update_slice_in_dim(ready, all_values, (back - rr) % prior *...]
    all_gather x1 -> x0, blocking collectives: 11.9 us -> none  [per_device(): second_factor = lax.all_gather(merge_q2[0], 'grp', axis=0, tiled=True)]
    ppermute x0 -> x7, starting transfers between devices: none -> 8.68 us  [the longest x3 8.12 us: _produce_case(): finding = lax.ppermute(finding, axis_name='grp', perm=blocks_here)]
    psum x1, waiting for transfers between devices: 124 us -> 131 us  [per_device(): top_adjoint = -lax.psum(product(projected, combined, 0, 0), ('grp', 'top'))]
    ppermute x0 -> x7, waiting for transfers between devices: none -> 6.46 us  [the longest x4 5.54 us: _produce_case(): all_values = lax.ppermute(all_values, axis_name='grp', perm=table)]
  transfers between devices with their start and end apart: 1 -> 8, of which waited for: 1 -> 4; matrix products, arithmetic and copies ran while one was open for 1% -> 8% of each run, Pallas kernels for 0% -> 0%
where the time goes in v1:
time: 189 us; the launch traced here: 188 us
  waiting for transfers between devices  137 us (72%)
  local copies, waits for them, and re-layouts  16.8 us (9%)
  between operations  13.7 us (7%)
  matrix products  10.6 us (6%)
  starting transfers between devices  8.69 us (5%)
    psum x1, waiting for transfers between devices, per_device(): top_adjoint = -lax.psum(product(projected, combined, 0, 0), ('grp', 'top'))  131 us
    dot_general x7, matrix products, product(): lax.dot_general(former, latter, (((former_dim,), (latter_dim,)), ((), ())...  10.6 us
    ppermute x3, starting transfers between devices, _produce_case(): finding = lax.ppermute(finding, axis_name='grp', perm=blocks_here)  8.12 us
    dynamic_update_slice x4, local copies, waits for them, and re-layouts, _produce_case(): lax.dynamic_update_slice_in_dim(ready, all_values, (back - rr) % prior *...  6.02 us
    dynamic_update_slice x3, local copies, waits for them, and re-layouts, _produce_case(): lax.dynamic_update_slice_in_dim(ready, finding, (back + rr) % prior * z,...  5.99 us
    ppermute x4, waiting for transfers between devices, _produce_case(): all_values = lax.ppermute(all_values, axis_name='grp', perm=table)  5.54 us
  transfers between devices with their start and end apart: 8, of which 4 were waited for; matrix products, arithmetic and copies ran while one was open for 8% of the time, Pallas kernels for 0%

profile of v1, /device:TPU:0, one launch (start us, length us, event | category | flops | bytes accessed | tf_op | source)
XLA Modules:
  0.0 188.5 jit_solution(12676799592542672888)
XLA Ops:
  6.5 1.1 copy.6
  7.6 0.5 collective-permute-start
  8.1 2.9 %collective-permute-start.1 = (f32[48,384]{0,1:T(8,128)S(1)}, f32[48,384]{0,1:T(8,128)S(1)}, u32[]{:S(2)}, u32[]{:S(2)}) collective-permute-start(f32[48,384]{0,1:T(8,128)S(1)} %bitcast.30), channel_id=1, source_target_pairs={{0,28},{4,0},{8,4},{12,8},{16,12},{20,16},{24,20},{28,24},{1,29},{... | collective-permute-start | bytes 221192 | tf_op jit(solution)/shard_map/ppermute | solution.py:28
  11.1 3.3 %collective-permute-done = f32[48,384]{0,1:T(8,128)S(1)} collective-permute-done((f32[48,384]{0,1:T(8,128)S(1)}, f32[48,384]{0,1:T(8,128)S(1)}, u32[]{:S(2)}, u32[]{:S(2)}) %collective-permute-start) | collective-permute-done | bytes 73760 | tf_op jit(solution)/shard_map/ppermute | solution.py:23
  14.4 0.1 collective-permute-start.2
  14.4 0.9 collective-permute-done.1
  15.3 2.8 %collective-permute-start.3 = (f32[48,384]{0,1:T(8,128)S(1)}, f32[48,384]{0,1:T(8,128)S(1)}, u32[]{:S(2)}, u32[]{:S(2)}) collective-permute-start(f32[48,384]{0,1:T(8,128)S(1)} %collective-permute-done.1), channel_id=1, source_target_pairs={{0,28},{4,0},{8,4},{12,8},{16,12},{20,16},{24,20},{28,24},{1,29},{... | collective-permute-start | bytes 221192 | tf_op jit(solution)/shard_map/ppermute | solution.py:28
  18.1 2.2 %collective-permute-done.2 = f32[48,384]{0,1:T(8,128)S(1)} collective-permute-done((f32[48,384]{0,1:T(8,128)S(1)}, f32[48,384]{0,1:T(8,128)S(1)}, u32[]{:S(2)}, u32[]{:S(2)}) %collective-permute-start.2) | collective-permute-done | bytes 73760 | tf_op jit(solution)/shard_map/ppermute | solution.py:23
  20.4 1.9 %fusion = f32[384,384]{1,0:T(8,128)S(1)} fusion(f32[1,1,512,384]{3,2,1,0:T(8,128)S(1)} %copy-done, f32[1,1,512,384]{3,2,1,0:T(8,128)} %param.5), kind=kOutput, calls=%fused_computation.2 | convolution fusion | flops 452984832 | bytes 2162688 | tf_op jit(solution)/shard_map/dot_general | solution.py:39
  22.5 1.5 dynamic_update_slice.24
  24.1 2.4 %collective-permute-start.5 = (f32[48,384]{0,1:T(8,128)S(1)}, f32[48,384]{0,1:T(8,128)}, u32[]{:S(2)}, u32[]{:S(2)}) collective-permute-start(f32[48,384]{0,1:T(8,128)S(1)} %collective-permute-done.3), channel_id=1, source_target_pairs={{0,28},{4,0},{8,4},{12,8},{16,12},{20,16},{24,20},{28,24},{1,29},{... | collective-permute-start | bytes 221192 | tf_op jit(solution)/shard_map/ppermute | solution.py:28
  26.5 1.2 dynamic_update_slice.25
  27.7 1.8 dynamic_update_slice.26
  29.5 1.2 dynamic_update_slice.27
  30.7 1.8 dynamic_update_slice.28
  32.5 0.0 copy-start.2
  32.5 1.8 dynamic_update_slice.29
  34.4 2.3 %dynamic_update_slice.30 = f32[384,384]{0,1:T(8,128)S(1)} dynamic-update-slice(f32[384,384]{0,1:T(8,128)S(1)} %dynamic_update_slice.29, f32[48,384]{0,1:T(8,128)} %collective-permute-done.5, s32[]{:T(128)S(6)} %select_n.75, s32[]{:T(128)} %constant.60.clone.1) | dynamic-update-slice | bytes 147460 | tf_op jit(solution)/shard_map/dynamic_update_slice | solution.py:29
  36.7 1.8 dynamic_update_slice.31
  38.6 0.7 fusion.7
  39.3 1.9 %fusion.16 = f32[384,384]{1,0:T(8,128)} fusion(f32[384,384]{1,0:T(8,128)S(1)} %fusion, f32[384,384]{1,0:T(8,128)S(1)} %fusion.7), kind=kOutput, calls=%fused_computation.22 | convolution fusion | flops 339738624 | bytes 1769472 | tf_op jit(solution)/shard_map/dot_general | solution.py:39
  41.3 0.0 all-reduce.2.cloned.1.call-update
  41.3 1.0 copy-done.3
  42.3 0.7 fusion.5
  43.0 0.8 fusion.2
  43.9 131.0 %all-reduce.2.cloned.1.call-done = f32[384,384]{1,0:T(8,128)} async-done(((f32[384,384]{1,0:T(8,128)}), f32[384,384]{1,0:T(8,128)}) %all-reduce.2.cloned.1.call-update) | async-done | bytes 589840 | tf_op jit(solution)/shard_map/psum | solution.py:60
  174.9 1.1 neg.3
  176.0 0.0 copy-start.1
  176.0 1.1 copy.7
  177.1 0.1 copy-done.1
  177.1 2.7 %convolution_add_fusion = f32[512,384]{1,0:T(8,128)S(1)} fusion(f32[384,512]{1,0:T(8,128)S(1)} %fusion.2, f32[1,1,512,384]{3,2,1,0:T(8,128)S(1)} %copy-done.1, f32[384,384]{0,1:T(8,128)} %copy.7, s32[384]{0:T(512)S(1)} %iota_add_fusion, f32[384,384]{1,0:T(8,128)} %all-reduce.2.cloned.1.call-done), kind=kOutput, calls=%fused_computation.1 | convolution fusion | flops 454066176 | bytes 3540480 | tf_op jit(solution)/shard_map/dot_general | solution.py:39
  179.9 1.8 convolution_bitcast_fusion
  (13 shorter events, 0.1 us)
Async XLA Ops:
  6.5 13.9 %copy-start = (f32[1,1,512,384]{3,2,1,0:T(8,128)S(1)}, f32[1,1,512,384]{3,2,1,0:T(8,128)}, u32[]{:S(2)}) copy-start(f32[1,1,512,384]{3,2,1,0:T(8,128)} %param.6) | copy-start | bytes 2359300
  6.5 168.4 %all-reduce.2.cloned.1.call-start = ((), (), s32[]{:S(2)}) async-start(), calls=%async_computation | async-start | bytes 1179648 | tf_op jit(solution)/shard_map/psum | solution.py:60
  7.6 6.7 %collective-permute-start = (f32[48,384]{0,1:T(8,128)S(1)}, f32[48,384]{0,1:T(8,128)S(1)}, u32[]{:S(2)}, u32[]{:S(2)}) collective-permute-start(f32[48,384]{0,1:T(8,128)S(1)} %bitcast.29), channel_id=1, source_target_pairs={{0,4},{4,8},{8,12},{12,16},{16,20},{20,24},{24,28},{28,0},{1,5},{5... | collective-permute-start | bytes 221192 | tf_op jit(solution)/shard_map/ppermute | solution.py:23
  8.1 7.2 %collective-permute-start.1 = (f32[48,384]{0,1:T(8,128)S(1)}, f32[48,384]{0,1:T(8,128)S(1)}, u32[]{:S(2)}, u32[]{:S(2)}) collective-permute-start(f32[48,384]{0,1:T(8,128)S(1)} %bitcast.30), channel_id=1, source_target_pairs={{0,28},{4,0},{8,4},{12,8},{16,12},{20,16},{24,20},{28,24},{1,29},{... | collective-permute-start | bytes 221192 | tf_op jit(solution)/shard_map/ppermute | solution.py:28
  14.4 6.0 %collective-permute-start.2 = (f32[48,384]{0,1:T(8,128)S(1)}, f32[48,384]{0,1:T(8,128)S(1)}, u32[]{:S(2)}, u32[]{:S(2)}) collective-permute-start(f32[48,384]{0,1:T(8,128)S(1)} %collective-permute-done), channel_id=1, source_target_pairs={{0,4},{4,8},{8,12},{12,16},{16,20},{20,24},{24,28},{28,0},{1,5},{5... | collective-permute-start | bytes 221192 | tf_op jit(solution)/shard_map/ppermute | solution.py:23
  15.3 8.8 %collective-permute-start.3 = (f32[48,384]{0,1:T(8,128)S(1)}, f32[48,384]{0,1:T(8,128)S(1)}, u32[]{:S(2)}, u32[]{:S(2)}) collective-permute-start(f32[48,384]{0,1:T(8,128)S(1)} %collective-permute-done.1), channel_id=1, source_target_pairs={{0,28},{4,0},{8,4},{12,8},{16,12},{20,16},{24,20},{28,24},{1,29},{... | collective-permute-start | bytes 221192 | tf_op jit(solution)/shard_map/ppermute | solution.py:28
  20.4 6.1 %collective-permute-start.4 = (f32[48,384]{0,1:T(8,128)S(1)}, f32[48,384]{0,1:T(8,128)S(1)}, u32[]{:S(2)}, u32[]{:S(2)}) collective-permute-start(f32[48,384]{0,1:T(8,128)S(1)} %collective-permute-done.2), channel_id=1, source_target_pairs={{0,4},{4,8},{8,12},{12,16},{16,20},{20,24},{24,28},{28,0},{1,5},{5... | collective-permute-start | bytes 221192 | tf_op jit(solution)/shard_map/ppermute | solution.py:23
  24.1 10.3 %collective-permute-start.5 = (f32[48,384]{0,1:T(8,128)S(1)}, f32[48,384]{0,1:T(8,128)}, u32[]{:S(2)}, u32[]{:S(2)}) collective-permute-start(f32[48,384]{0,1:T(8,128)S(1)} %collective-permute-done.3), channel_id=1, source_target_pairs={{0,28},{4,0},{8,4},{12,8},{16,12},{20,16},{24,20},{28,24},{1,29},{... | collective-permute-start | bytes 221192 | tf_op jit(solution)/shard_map/ppermute | solution.py:28
  26.5 10.3 %collective-permute-start.6 = (f32[48,384]{0,1:T(8,128)S(1)}, f32[48,384]{0,1:T(8,128)S(1)}, u32[]{:S(2)}, u32[]{:S(2)}) collective-permute-start(f32[48,384]{0,1:T(8,128)S(1)} %collective-permute-done.4), channel_id=1, source_target_pairs={{0,4},{4,8},{8,12},{12,16},{16,20},{20,24},{24,28},{28,0},{1,5},{5... | collective-permute-start | bytes 221192 | tf_op jit(solution)/shard_map/ppermute | solution.py:23
  32.5 6.1 %copy-start.2 = (f32[1,1,384,384]{3,2,1,0:T(8,128)S(1)}, f32[1,1,384,384]{3,2,1,0:T(8,128)}, u32[]{:S(2)}) copy-start(f32[1,1,384,384]{3,2,1,0:T(8,128)} %param.8) | copy-start | bytes 1769476
  41.3 1.1 copy-start.3
  176.0 1.1 copy-start.1
Sparse Core Ops, SparseCore 0:
  41.4 133.4 all-reduce.1
